TPU v7x, 128 devices: a whole 4x4x4 slice. The times are simulated.
128 devices in a mesh: ocean: 2 (over core), ice: 64 (over z, y, x).
Axes of the slice: x: 4, y: 4, z: 4, core: 2. Of those that a mesh axis runs over, the one named last changes fastest.
Arguments:
- velocity: float32 [128, 512, 128], P('ocean', 'ice'), may hold values from -6 to 6
- stress: float32 [128, 512, 128], P('ocean', 'ice'), may hold values from -6 to 6
- thickness: float32 [128, 512, 128], P('ocean', 'ice'), may hold values from 0.5 to 2
- forcing: float32 [128, 512, 128], P('ocean', 'ice'), may hold values from -6 to 6
- switch: int32 [128, 512, 128], P('ocean', 'ice'), may hold values 0 or 1
- covered: int32 [128], P('ocean'), may hold values from 0 to 1, as said below
- reinit: int32 [128], P('ocean'), may hold values 0 or 1
- cot_velocity: float32 [128, 512, 128], P('ocean', 'ice'), may hold values from -6 to 6
- cot_stress: float32 [128, 512, 128], P('ocean', 'ice'), may hold values from -6 to 6
- kernel: float32 [512, 512], replicated, may hold values from 0 to 1, as said below
Outputs:
- grad_velocity: float32 [128, 512, 128], P('ocean', 'ice')
- grad_stress: float32 [128, 512, 128], P('ocean', 'ice')
- grad_thickness: float32 [128, 512, 128], P('ocean', 'ice')
- grad_forcing: float32 [128, 512, 128], P('ocean', 'ice')
Inputs may be any that keep to these rules, and one draw needn't show every extreme that they name: Exactly 32 blocks are covered; one index of ocean holds 31 of them and the other holds one. The kernel's diagonal exceeds the sum of each row's other entries.
All inputs are finite; a program needn't handle non-finite values. No bound on the sum of `switch` or of `reinit` on one device may be relied on, other than what follows from the above.
Results may differ from a plain program's by a relative error of at most 0.00015.
Values sent between devices are 32-bit elements; how exact they have to be, the bound alone decides.
No kernel may reach another device: no remote copies, remote signals or barrier semaphores. Data moves between devices by JAX's collectives and lax.ppermute only.
A program may use at most 64 MiB of HBM per device.

v0:
```python
import jax
import jax.numpy as jnp
from jax import lax
from jax.sharding import PartitionSpec as P

SUB = 8
WINDOWS = 2
PLASTIC = 0.25
VISCOUS = 1.0
GAMMA = 0.6
BETA = 0.9
STEP = 0.04


def passed_along(block, axis, distance):
    devices = range(lax.axis_size(axis))
    route = [(i - distance, i) for i in devices if i - distance in devices]
    return lax.ppermute(block, axis, route)


def prefix(part, axis, combine, identity):
    place = lax.axis_index(axis)
    gathered = lax.all_gather(part, axis)
    state = jnp.zeros_like(part) + jnp.asarray(identity, part.dtype)

    def one(turn, state):
        return combine(state, lax.dynamic_index_in_dim(gathered, turn, 0, False))

    return lax.fori_loop(0, place, one, state)


def forward_diff(x):
    above = passed_along(x[:, -1:], "ice", 1)
    upper = jnp.concatenate([above, x[:, :-1]], axis=1)
    left = jnp.pad(x, ((0, 0), (0, 0), (1, 0)))[:, :, :-1]
    return 2.0 * x - upper - left


def backward_diff(x):
    below = passed_along(x[:, :1], "ice", -1)
    lower = jnp.concatenate([x[:, 1:], below], axis=1)
    right = jnp.pad(x, ((0, 0), (0, 0), (0, 1)))[:, :, 1:]
    return 2.0 * x - lower - right


def ice_work(velo, stress_now, source, force, cot_u, cot_s, keep, kernel):
    rows_dev = velo.shape[1]
    first = lax.axis_index("ice") * rows_dev
    own_rows = lax.dynamic_slice_in_dim(kernel, first, rows_dev, 0)
    own_cols = lax.dynamic_slice_in_dim(kernel, first, rows_dev, 1)
    zeta = jnp.einsum(
        "ij,wjc->wic",
        own_rows,
        lax.all_gather(source, "ice", axis=1, tiled=True),
        precision=lax.Precision.HIGHEST,
    )
    scale = keep[:, None, None]

    def advance(carry, unused):
        u_now, s_now = carry
        strain = forward_diff(u_now)
        s_now = GAMMA * s_now + zeta * strain
        u_now = BETA * u_now - STEP * backward_diff(s_now) + STEP * force
        return ((u_now, s_now), strain)

    u_now, s_now = (velo, stress_now)
    strains = []
    for window in range(WINDOWS):
        if window > 0:
            s_now = s_now * scale
        (u_now, s_now), saved = lax.scan(advance, (u_now, s_now), None, length=SUB)
        strains.append(saved)

    def retreat(carry, strain):
        adj_u, adj_s, adj_z, adj_f = carry
        total_s = adj_s - STEP * forward_diff(adj_u)
        adj_f = adj_f + STEP * adj_u
        adj_u = BETA * adj_u + backward_diff(zeta * total_s)
        adj_z = adj_z + total_s * strain
        adj_s = GAMMA * total_s
        return ((adj_u, adj_s, adj_z, adj_f), None)

    zeros = jnp.zeros_like(velo)
    carry = (cot_u, cot_s, zeros, zeros)
    for window in range(WINDOWS - 1, -1, -1):
        carry, unused = lax.scan(retreat, carry, strains[window], reverse=True)
        if window > 0:
            carry = (carry[0], carry[1] * scale, carry[2], carry[3])
    adj_u, adj_s, adj_z, adj_f = carry
    adj_q = jnp.einsum(
        "ij,wic->wjc",
        own_cols,
        lax.all_gather(adj_z, "ice", axis=1, tiled=True),
        precision=lax.Precision.HIGHEST,
    )
    return (adj_u, adj_s, adj_q, adj_f)


def shards(
    velocity, stress, thickness, forcing, switch, covered, reinit, cot_velocity, cot_stress, kernel
):
    coef = jnp.where(switch == 1, PLASTIC, VISCOUS).astype(jnp.float32)
    source = thickness * coef
    keep = (1 - reinit).astype(jnp.float32)
    live = covered.astype(jnp.float32)[:, None, None]
    blocks = covered.shape[0]
    work = blocks // 4
    peers = lax.axis_size("ocean")
    cap = (min(blocks, work * peers) + peers - 1) // peers
    count = jnp.sum(covered)
    offset = prefix(count, "ocean", lambda early, late: early + late, jnp.int32(0))
    rank = jnp.cumsum(covered) - covered
    slot_ids = jnp.arange(peers * cap, dtype=jnp.int32)
    owner_of = slot_ids // cap
    place_of = slot_ids % cap
    wanted = place_of * peers + (owner_of - offset) % peers
    valid = wanted < count
    match = (covered[None, :] == 1) & (rank[None, :] == wanted[:, None])
    source_idx = jnp.sum(jnp.where(match, jnp.arange(blocks, dtype=jnp.int32)[None, :], 0), axis=1)
    work_slot = jnp.where(valid, (offset + wanted) // peers, -1).astype(jnp.float32)
    stacked = jnp.stack([velocity, stress, source, forcing, cot_velocity, cot_stress], axis=1)
    validf = valid.astype(jnp.float32)
    packed = jnp.take(stacked, source_idx, axis=0) * validf[:, None, None, None]
    keep_send = jnp.take(keep, source_idx, axis=0) * validf
    arrived, keep_recv, slot_recv = (
        lax.all_to_all(packed, "ocean", split_axis=0, concat_axis=0, tiled=True),
        lax.all_to_all(keep_send, "ocean", split_axis=0, concat_axis=0, tiled=True),
        lax.all_to_all(work_slot, "ocean", split_axis=0, concat_axis=0, tiled=True),
    )
    slot_int = slot_recv.astype(jnp.int32)
    picks = slot_int[None, :] == jnp.arange(work, dtype=jnp.int32)[:, None]
    pick_idx = jnp.sum(
        jnp.where(picks, jnp.arange(slot_int.shape[0], dtype=jnp.int32)[None, :], 0), axis=1
    )
    fields = jnp.take(arrived, pick_idx, axis=0)
    keep_work = jnp.take(keep_recv, pick_idx, axis=0)
    results = ice_work(
        fields[:, 0],
        fields[:, 1],
        fields[:, 2],
        fields[:, 3],
        fields[:, 4],
        fields[:, 5],
        keep_work,
        kernel,
    )
    gathered = jnp.stack(results, axis=1)
    present = (slot_int >= 0).astype(jnp.float32)
    outgoing = (
        jnp.take(gathered, jnp.clip(slot_int, 0, work - 1), axis=0) * present[:, None, None, None]
    )
    returned = lax.all_to_all(outgoing, "ocean", split_axis=0, concat_axis=0, tiled=True)
    global_idx = offset + rank
    home_slot = global_idx % peers * cap + rank // peers
    mine = jnp.take(returned, jnp.clip(home_slot, 0, peers * cap - 1), axis=0)
    grad_u, grad_s, grad_q, grad_f = (mine[:, 0], mine[:, 1], mine[:, 2], mine[:, 3])
    return (grad_u * live, grad_s * live, grad_q * coef * live, grad_f * live)


def solution(mesh):
    placed = (
        P("ocean", "ice", None),
        P("ocean", "ice", None),
        P("ocean", "ice", None),
        P("ocean", "ice", None),
        P("ocean", "ice", None),
        P("ocean"),
        P("ocean"),
        P("ocean", "ice", None),
        P("ocean", "ice", None),
        P(),
    )
    return jax.shard_map(
        shards,
        mesh=mesh,
        in_specs=placed,
        out_specs=(
            P("ocean", "ice", None),
            P("ocean", "ice", None),
            P("ocean", "ice", None),
            P("ocean", "ice", None),
        ),
        check_vma=False,
    )
```

profile of v0, /device:TPU:1, one launch (start us, length us, event | category | flops | bytes accessed | tf_op | source)
XLA Modules:
  0.0 721.2 jit_solution(8110284426354356338)
XLA Ops:
  45.0 77.3 %all-gather.6.cloned.1.call-done = f32[16,1,512,128]{3,2,0,1:T(8,128)} async-done(((f32[16,1,8,128]{3,2,0,1:T(8,128)}), f32[16,1,512,128]{3,2,0,1:T(8,128)}) %all-gather.6.cloned.1.call-update) | async-done | bytes 4194320 | tf_op jit(solution)/shard_map/all_gather | solution.py:54
  126.7 84.1 %while.84 = (s32[]{:T(128)}, f32[16,8,128]{2,1,0:T(8,128)S(1)}, f32[16,8,128]{2,1,0:T(8,128)S(1)}, f32[8,16,8,128]{3,2,1,0:T(8,128)S(1)}, f32[16,8,128]{2,1,0:T(...) while((s32[]{:T(128)}, f32[16,8,128]{2,1,0:T(8,128)S(1)}, f32[16,8,128]{2,1,0:T(8,128)S(1)}, ...), condition=%wide.region_7.8_spmd, body=%wide.region_6.7_spmd.sunk | while | flops 262146 | bytes 1073313 | solution.py:71
  154.7 5.5 collective-permute-start
  199.7 5.5 collective-permute-start
  211.0 90.0 %while.85 = (s32[]{:T(128)}, f32[16,8,128]{2,1,0:T(8,128)S(1)}, f32[16,8,128]{2,1,0:T(8,128)S(1)}, f32[8,16,8,128]{3,2,1,0:T(8,128)S(1)}, f32[16,8,128]{2,1,0:T(...) while((s32[]{:T(128)}, f32[16,8,128]{2,1,0:T(8,128)S(1)}, f32[16,8,128]{2,1,0:T(8,128)S(1)}, ...), condition=%wide.region_9.10_spmd, body=%wide.region_8.9_spmd.sunk | while | flops 262146 | bytes 1073313 | solution.py:71
  301.0 104.9 %while.87 = (s32[]{:T(128)}, f32[16,8,128]{2,1,0:T(8,128)S(1)}, f32[16,8,128]{2,1,0:T(8,128)S(1)}, f32[16,8,128]{2,1,0:T(8,128)S(1)}, f32[16,8,128]{2,1,0:T(8,12...) while((s32[]{:T(128)}, f32[16,8,128]{2,1,0:T(8,128)S(1)}, ...), condition=%wide.region_11.12_spmd.clone, body=%wide.region_10.11_spmd.clone.sunk | while | flops 327684 | bytes 1327311 | solution.py:86
  301.0 5.5 collective-permute-start.6
  312.8 7.3 %collective-permute-start.6 = (f32[16,1,128]{2,1,0:T(1,128)S(1)}, f32[16,1,128]{2,1,0:T(1,128)S(1)}, u32[]{:S(2)}, u32[]{:S(2)}) collective-permute-start(f32[16,1,128]{2,1,0:T(1,128)S(1)} %slice.355), channel_id=1, source_target_pairs={{0,1},{1,2},{2,3},{3,4},{4,5},{5,6},{6,7},{7,8},{8,9},{9,10},{10,1... | collective-permute-start | bytes 24584 | tf_op jit(solution)/shard_map/while/body/eval_jaxpr/ppermute | solution.py:18
  326.3 7.1 collective-permute-start.6
  339.0 7.8 %collective-permute-start.6 = (f32[16,1,128]{2,1,0:T(1,128)S(1)}, f32[16,1,128]{2,1,0:T(1,128)S(1)}, u32[]{:S(2)}, u32[]{:S(2)}) collective-permute-start(f32[16,1,128]{2,1,0:T(1,128)S(1)} %slice.355), channel_id=1, source_target_pairs={{0,1},{1,2},{2,3},{3,4},{4,5},{5,6},{6,7},{7,8},{8,9},{9,10},{10,1... | collective-permute-start | bytes 24584 | tf_op jit(solution)/shard_map/while/body/eval_jaxpr/ppermute | solution.py:18
  352.5 7.4 %collective-permute-start.6 = (f32[16,1,128]{2,1,0:T(1,128)S(1)}, f32[16,1,128]{2,1,0:T(1,128)S(1)}, u32[]{:S(2)}, u32[]{:S(2)}) collective-permute-start(f32[16,1,128]{2,1,0:T(1,128)S(1)} %slice.355), channel_id=1, source_target_pairs={{0,1},{1,2},{2,3},{3,4},{4,5},{5,6},{6,7},{7,8},{8,9},{9,10},{10,1... | collective-permute-start | bytes 24584 | tf_op jit(solution)/shard_map/while/body/eval_jaxpr/ppermute | solution.py:18
  365.8 7.6 %collective-permute-start.6 = (f32[16,1,128]{2,1,0:T(1,128)S(1)}, f32[16,1,128]{2,1,0:T(1,128)S(1)}, u32[]{:S(2)}, u32[]{:S(2)}) collective-permute-start(f32[16,1,128]{2,1,0:T(1,128)S(1)} %slice.355), channel_id=1, source_target_pairs={{0,1},{1,2},{2,3},{3,4},{4,5},{5,6},{6,7},{7,8},{8,9},{9,10},{10,1... | collective-permute-start | bytes 24584 | tf_op jit(solution)/shard_map/while/body/eval_jaxpr/ppermute | solution.py:18
  379.4 7.2 %collective-permute-start.6 = (f32[16,1,128]{2,1,0:T(1,128)S(1)}, f32[16,1,128]{2,1,0:T(1,128)S(1)}, u32[]{:S(2)}, u32[]{:S(2)}) collective-permute-start(f32[16,1,128]{2,1,0:T(1,128)S(1)} %slice.355), channel_id=1, source_target_pairs={{0,1},{1,2},{2,3},{3,4},{4,5},{5,6},{6,7},{7,8},{8,9},{9,10},{10,1... | collective-permute-start | bytes 24584 | tf_op jit(solution)/shard_map/while/body/eval_jaxpr/ppermute | solution.py:18
  392.6 7.3 %collective-permute-start.6 = (f32[16,1,128]{2,1,0:T(1,128)S(1)}, f32[16,1,128]{2,1,0:T(1,128)S(1)}, u32[]{:S(2)}, u32[]{:S(2)}) collective-permute-start(f32[16,1,128]{2,1,0:T(1,128)S(1)} %slice.355), channel_id=1, source_target_pairs={{0,1},{1,2},{2,3},{3,4},{4,5},{5,6},{6,7},{7,8},{8,9},{9,10},{10,1... | collective-permute-start | bytes 24584 | tf_op jit(solution)/shard_map/while/body/eval_jaxpr/ppermute | solution.py:18
  406.0 107.0 %while.86 = (s32[]{:T(128)}, f32[16,8,128]{2,1,0:T(8,128)S(1)}, f32[16,8,128]{2,1,0:T(8,128)S(1)}, f32[16,8,128]{2,1,0:T(8,128)S(1)}, f32[16,8,128]{2,1,0:T(8,12...) while((s32[]{:T(128)}, f32[16,8,128]{2,1,0:T(8,128)S(1)}, ...), condition=%wide.region_13.14_spmd, body=%wide.region_12.13_spmd.sunk | while | flops 294915 | bytes 1327293 | solution.py:86
  406.0 7.6 %collective-permute-start.4 = (f32[16,1,128]{2,1,0:T(1,128)S(1)}, f32[16,1,128]{2,1,0:T(1,128)S(1)}, u32[]{:S(2)}, u32[]{:S(2)}) collective-permute-start(f32[16,1,128]{2,1,0:T(1,128)S(1)} %slice.351), channel_id=1, source_target_pairs={{0,1},{1,2},{2,3},{3,4},{4,5},{5,6},{6,7},{7,8},{8,9},{9,10},{10,1... | collective-permute-start | bytes 24584 | tf_op jit(solution)/shard_map/while/body/eval_jaxpr/ppermute | solution.py:18
  419.5 7.3 %collective-permute-start.4 = (f32[16,1,128]{2,1,0:T(1,128)S(1)}, f32[16,1,128]{2,1,0:T(1,128)S(1)}, u32[]{:S(2)}, u32[]{:S(2)}) collective-permute-start(f32[16,1,128]{2,1,0:T(1,128)S(1)} %slice.351), channel_id=1, source_target_pairs={{0,1},{1,2},{2,3},{3,4},{4,5},{5,6},{6,7},{7,8},{8,9},{9,10},{10,1... | collective-permute-start | bytes 24584 | tf_op jit(solution)/shard_map/while/body/eval_jaxpr/ppermute | solution.py:18
  432.8 7.6 %collective-permute-start.4 = (f32[16,1,128]{2,1,0:T(1,128)S(1)}, f32[16,1,128]{2,1,0:T(1,128)S(1)}, u32[]{:S(2)}, u32[]{:S(2)}) collective-permute-start(f32[16,1,128]{2,1,0:T(1,128)S(1)} %slice.351), channel_id=1, source_target_pairs={{0,1},{1,2},{2,3},{3,4},{4,5},{5,6},{6,7},{7,8},{8,9},{9,10},{10,1... | collective-permute-start | bytes 24584 | tf_op jit(solution)/shard_map/while/body/eval_jaxpr/ppermute | solution.py:18
  446.1 7.3 %collective-permute-start.4 = (f32[16,1,128]{2,1,0:T(1,128)S(1)}, f32[16,1,128]{2,1,0:T(1,128)S(1)}, u32[]{:S(2)}, u32[]{:S(2)}) collective-permute-start(f32[16,1,128]{2,1,0:T(1,128)S(1)} %slice.351), channel_id=1, source_target_pairs={{0,1},{1,2},{2,3},{3,4},{4,5},{5,6},{6,7},{7,8},{8,9},{9,10},{10,1... | collective-permute-start | bytes 24584 | tf_op jit(solution)/shard_map/while/body/eval_jaxpr/ppermute | solution.py:18
  459.4 7.6 %collective-permute-start.4 = (f32[16,1,128]{2,1,0:T(1,128)S(1)}, f32[16,1,128]{2,1,0:T(1,128)S(1)}, u32[]{:S(2)}, u32[]{:S(2)}) collective-permute-start(f32[16,1,128]{2,1,0:T(1,128)S(1)} %slice.351), channel_id=1, source_target_pairs={{0,1},{1,2},{2,3},{3,4},{4,5},{5,6},{6,7},{7,8},{8,9},{9,10},{10,1... | collective-permute-start | bytes 24584 | tf_op jit(solution)/shard_map/while/body/eval_jaxpr/ppermute | solution.py:18
  473.0 7.2 collective-permute-start.4
  486.2 7.3 %collective-permute-start.4 = (f32[16,1,128]{2,1,0:T(1,128)S(1)}, f32[16,1,128]{2,1,0:T(1,128)S(1)}, u32[]{:S(2)}, u32[]{:S(2)}) collective-permute-start(f32[16,1,128]{2,1,0:T(1,128)S(1)} %slice.351), channel_id=1, source_target_pairs={{0,1},{1,2},{2,3},{3,4},{4,5},{5,6},{6,7},{7,8},{8,9},{9,10},{10,1... | collective-permute-start | bytes 24584 | tf_op jit(solution)/shard_map/while/body/eval_jaxpr/ppermute | solution.py:18
  500.0 7.0 collective-permute-start.4
  513.7 188.2 %all-gather.4.cloned.1.call-done = f32[16,512,128]{2,1,0:T(8,128)} async-done(((f32[16,8,128]{2,1,0:T(8,128)}), f32[16,512,128]{2,1,0:T(8,128)}) %all-gather.4.cloned.1.call-update) | async-done | bytes 4194320 | tf_op jit(solution)/shard_map/all_gather | solution.py:93
  (391 shorter events, 313.1 us)
Async XLA Ops:
  16.8 16.8 %all-to-all-start = ((f32[2,16,1]{1,2,0:T(1,128)}), f32[2,16,1]{1,2,0:T(1,128)S(1)}, u32[]{:S(2)}, u32[]{:S(2)}) async-start(f32[2,16,1]{1,2,0:T(1,128)} %bitcast.7), calls=%async_computation | async-start | bytes 2048 | tf_op jit(solution)/shard_map/all_to_all | solution.py:128
  41.6 80.7 %all-gather.6.cloned.1.call-start = ((), (), s32[]{:S(2)}) async-start(), calls=%async_computation.5 | async-start | bytes 4259840 | tf_op jit(solution)/shard_map/all_gather | solution.py:54
  44.9 657.0 %all-gather.4.cloned.1.call-start = ((), (), s32[]{:S(2)}) async-start(), calls=%async_computation.4 | async-start | bytes 4259840 | tf_op jit(solution)/shard_map/all_gather | solution.py:93
  154.7 6.3 collective-permute-start
  166.2 6.3 collective-permute-start
  177.3 6.3 collective-permute-start
  199.7 6.3 collective-permute-start
  278.4 6.3 collective-permute-start.2
  301.0 6.3 collective-permute-start.6
  312.8 8.1 %collective-permute-start.6 = (f32[16,1,128]{2,1,0:T(1,128)S(1)}, f32[16,1,128]{2,1,0:T(1,128)S(1)}, u32[]{:S(2)}, u32[]{:S(2)}) collective-permute-start(f32[16,1,128]{2,1,0:T(1,128)S(1)} %slice.355), channel_id=1, source_target_pairs={{0,1},{1,2},{2,3},{3,4},{4,5},{5,6},{6,7},{7,8},{8,9},{9,10},{10,1... | collective-permute-start | bytes 24584 | tf_op jit(solution)/shard_map/while/body/eval_jaxpr/ppermute | solution.py:18
  326.3 7.8 %collective-permute-start.6 = (f32[16,1,128]{2,1,0:T(1,128)S(1)}, f32[16,1,128]{2,1,0:T(1,128)S(1)}, u32[]{:S(2)}, u32[]{:S(2)}) collective-permute-start(f32[16,1,128]{2,1,0:T(1,128)S(1)} %slice.355), channel_id=1, source_target_pairs={{0,1},{1,2},{2,3},{3,4},{4,5},{5,6},{6,7},{7,8},{8,9},{9,10},{10,1... | collective-permute-start | bytes 24584 | tf_op jit(solution)/shard_map/while/body/eval_jaxpr/ppermute | solution.py:18
  339.0 8.6 %collective-permute-start.6 = (f32[16,1,128]{2,1,0:T(1,128)S(1)}, f32[16,1,128]{2,1,0:T(1,128)S(1)}, u32[]{:S(2)}, u32[]{:S(2)}) collective-permute-start(f32[16,1,128]{2,1,0:T(1,128)S(1)} %slice.355), channel_id=1, source_target_pairs={{0,1},{1,2},{2,3},{3,4},{4,5},{5,6},{6,7},{7,8},{8,9},{9,10},{10,1... | collective-permute-start | bytes 24584 | tf_op jit(solution)/shard_map/while/body/eval_jaxpr/ppermute | solution.py:18
  352.5 8.1 %collective-permute-start.6 = (f32[16,1,128]{2,1,0:T(1,128)S(1)}, f32[16,1,128]{2,1,0:T(1,128)S(1)}, u32[]{:S(2)}, u32[]{:S(2)}) collective-permute-start(f32[16,1,128]{2,1,0:T(1,128)S(1)} %slice.355), channel_id=1, source_target_pairs={{0,1},{1,2},{2,3},{3,4},{4,5},{5,6},{6,7},{7,8},{8,9},{9,10},{10,1... | collective-permute-start | bytes 24584 | tf_op jit(solution)/shard_map/while/body/eval_jaxpr/ppermute | solution.py:18
  365.8 8.4 %collective-permute-start.6 = (f32[16,1,128]{2,1,0:T(1,128)S(1)}, f32[16,1,128]{2,1,0:T(1,128)S(1)}, u32[]{:S(2)}, u32[]{:S(2)}) collective-permute-start(f32[16,1,128]{2,1,0:T(1,128)S(1)} %slice.355), channel_id=1, source_target_pairs={{0,1},{1,2},{2,3},{3,4},{4,5},{5,6},{6,7},{7,8},{8,9},{9,10},{10,1... | collective-permute-start | bytes 24584 | tf_op jit(solution)/shard_map/while/body/eval_jaxpr/ppermute | solution.py:18
  379.4 8.0 %collective-permute-start.6 = (f32[16,1,128]{2,1,0:T(1,128)S(1)}, f32[16,1,128]{2,1,0:T(1,128)S(1)}, u32[]{:S(2)}, u32[]{:S(2)}) collective-permute-start(f32[16,1,128]{2,1,0:T(1,128)S(1)} %slice.355), channel_id=1, source_target_pairs={{0,1},{1,2},{2,3},{3,4},{4,5},{5,6},{6,7},{7,8},{8,9},{9,10},{10,1... | collective-permute-start | bytes 24584 | tf_op jit(solution)/shard_map/while/body/eval_jaxpr/ppermute | solution.py:18
  392.6 8.0 %collective-permute-start.6 = (f32[16,1,128]{2,1,0:T(1,128)S(1)}, f32[16,1,128]{2,1,0:T(1,128)S(1)}, u32[]{:S(2)}, u32[]{:S(2)}) collective-permute-start(f32[16,1,128]{2,1,0:T(1,128)S(1)} %slice.355), channel_id=1, source_target_pairs={{0,1},{1,2},{2,3},{3,4},{4,5},{5,6},{6,7},{7,8},{8,9},{9,10},{10,1... | collective-permute-start | bytes 24584 | tf_op jit(solution)/shard_map/while/body/eval_jaxpr/ppermute | solution.py:18
  406.0 8.4 %collective-permute-start.4 = (f32[16,1,128]{2,1,0:T(1,128)S(1)}, f32[16,1,128]{2,1,0:T(1,128)S(1)}, u32[]{:S(2)}, u32[]{:S(2)}) collective-permute-start(f32[16,1,128]{2,1,0:T(1,128)S(1)} %slice.351), channel_id=1, source_target_pairs={{0,1},{1,2},{2,3},{3,4},{4,5},{5,6},{6,7},{7,8},{8,9},{9,10},{10,1... | collective-permute-start | bytes 24584 | tf_op jit(solution)/shard_map/while/body/eval_jaxpr/ppermute | solution.py:18
  419.5 8.1 %collective-permute-start.4 = (f32[16,1,128]{2,1,0:T(1,128)S(1)}, f32[16,1,128]{2,1,0:T(1,128)S(1)}, u32[]{:S(2)}, u32[]{:S(2)}) collective-permute-start(f32[16,1,128]{2,1,0:T(1,128)S(1)} %slice.351), channel_id=1, source_target_pairs={{0,1},{1,2},{2,3},{3,4},{4,5},{5,6},{6,7},{7,8},{8,9},{9,10},{10,1... | collective-permute-start | bytes 24584 | tf_op jit(solution)/shard_map/while/body/eval_jaxpr/ppermute | solution.py:18
  432.8 8.4 %collective-permute-start.4 = (f32[16,1,128]{2,1,0:T(1,128)S(1)}, f32[16,1,128]{2,1,0:T(1,128)S(1)}, u32[]{:S(2)}, u32[]{:S(2)}) collective-permute-start(f32[16,1,128]{2,1,0:T(1,128)S(1)} %slice.351), channel_id=1, source_target_pairs={{0,1},{1,2},{2,3},{3,4},{4,5},{5,6},{6,7},{7,8},{8,9},{9,10},{10,1... | collective-permute-start | bytes 24584 | tf_op jit(solution)/shard_map/while/body/eval_jaxpr/ppermute | solution.py:18
  446.1 8.1 %collective-permute-start.4 = (f32[16,1,128]{2,1,0:T(1,128)S(1)}, f32[16,1,128]{2,1,0:T(1,128)S(1)}, u32[]{:S(2)}, u32[]{:S(2)}) collective-permute-start(f32[16,1,128]{2,1,0:T(1,128)S(1)} %slice.351), channel_id=1, source_target_pairs={{0,1},{1,2},{2,3},{3,4},{4,5},{5,6},{6,7},{7,8},{8,9},{9,10},{10,1... | collective-permute-start | bytes 24584 | tf_op jit(solution)/shard_map/while/body/eval_jaxpr/ppermute | solution.py:18
  459.4 8.4 %collective-permute-start.4 = (f32[16,1,128]{2,1,0:T(1,128)S(1)}, f32[16,1,128]{2,1,0:T(1,128)S(1)}, u32[]{:S(2)}, u32[]{:S(2)}) collective-permute-start(f32[16,1,128]{2,1,0:T(1,128)S(1)} %slice.351), channel_id=1, source_target_pairs={{0,1},{1,2},{2,3},{3,4},{4,5},{5,6},{6,7},{7,8},{8,9},{9,10},{10,1... | collective-permute-start | bytes 24584 | tf_op jit(solution)/shard_map/while/body/eval_jaxpr/ppermute | solution.py:18
  473.0 8.0 %collective-permute-start.4 = (f32[16,1,128]{2,1,0:T(1,128)S(1)}, f32[16,1,128]{2,1,0:T(1,128)S(1)}, u32[]{:S(2)}, u32[]{:S(2)}) collective-permute-start(f32[16,1,128]{2,1,0:T(1,128)S(1)} %slice.351), channel_id=1, source_target_pairs={{0,1},{1,2},{2,3},{3,4},{4,5},{5,6},{6,7},{7,8},{8,9},{9,10},{10,1... | collective-permute-start | bytes 24584 | tf_op jit(solution)/shard_map/while/body/eval_jaxpr/ppermute | solution.py:18
  486.2 8.1 %collective-permute-start.4 = (f32[16,1,128]{2,1,0:T(1,128)S(1)}, f32[16,1,128]{2,1,0:T(1,128)S(1)}, u32[]{:S(2)}, u32[]{:S(2)}) collective-permute-start(f32[16,1,128]{2,1,0:T(1,128)S(1)} %slice.351), channel_id=1, source_target_pairs={{0,1},{1,2},{2,3},{3,4},{4,5},{5,6},{6,7},{7,8},{8,9},{9,10},{10,1... | collective-permute-start | bytes 24584 | tf_op jit(solution)/shard_map/while/body/eval_jaxpr/ppermute | solution.py:18
  500.0 7.8 %collective-permute-start.4 = (f32[16,1,128]{2,1,0:T(1,128)S(1)}, f32[16,1,128]{2,1,0:T(1,128)S(1)}, u32[]{:S(2)}, u32[]{:S(2)}) collective-permute-start(f32[16,1,128]{2,1,0:T(1,128)S(1)} %slice.351), channel_id=1, source_target_pairs={{0,1},{1,2},{2,3},{3,4},{4,5},{5,6},{6,7},{7,8},{8,9},{9,10},{10,1... | collective-permute-start | bytes 24584 | tf_op jit(solution)/shard_map/while/body/eval_jaxpr/ppermute | solution.py:18
  (52 other events, 436.5 us)
Sparse Core Ops, SparseCore 0:
  45.7 76.5 all-gather.5
  513.7 188.1 all-gather.3
where the time goes:
time: 724 us; the launch traced here: 721 us
  waiting for transfers between devices  403 us (56%)
  starting transfers between devices  248 us (34%)
  local copies, waits for them, and re-layouts  17.8 us (2%)
  other arithmetic  17.4 us (2%)
  between operations  14.4 us (2%)
  matrix products  8.86 us (1%)
  blocking collectives  8.21 us (1%)
    ppermute x64, starting transfers between devices, passed_along(): return lax.ppermute(block, axis, route)  238 us
    all_gather x1, waiting for transfers between devices, ice_work(): lax.all_gather(adj_z, 'ice', axis=1, tiled=True)  188 us
    ppermute x64, waiting for transfers between devices, passed_along(): return lax.ppermute(block, axis, route)  138 us
    all_gather x1, waiting for transfers between devices, ice_work(): lax.all_gather(source, 'ice', axis=1, tiled=True)  77.3 us
  transfers between devices with their start and end apart: 69, of which 66 were waited for; matrix products, arithmetic and copies ran while one was open for 2% of the time, Pallas kernels for 0%

commit v1 on v0

--- a/solution.py
+++ b/solution.py
@@ -2,6 +2,7 @@
 import jax.numpy as jnp
 from jax import lax
 from jax.sharding import PartitionSpec as P
+from jax.lax import all_to_all, axis_size
 
 SUB = 8
 WINDOWS = 2
@@ -87,10 +88,19 @@
         if window > 0:
             carry = (carry[0], carry[1] * scale, carry[2], carry[3])
     adj_u, adj_s, adj_z, adj_f = carry
+
+    def switch_views(here_x, chip_axis):
+        degree = axis_size(chip_axis)
+        item_now = range(here_x.ndim)
+        vals = list(map(lambda h: degree if h == 1 else 1, item_now))
+        return all_to_all(
+            jnp.tile(here_x, vals), chip_axis, split_axis=1, concat_axis=1, tiled=True
+        )
+
     adj_q = jnp.einsum(
         "ij,wic->wjc",
         own_cols,
-        lax.all_gather(adj_z, "ice", axis=1, tiled=True),
+        switch_views(adj_z, chip_axis="ice"),
         precision=lax.Precision.HIGHEST,
     )
     return (adj_u, adj_s, adj_q, adj_f)

time: 724 us -> 694 us (0.959)
  waiting for transfers between devices: 403 us -> 246 us
  blocking collectives: 8.21 us -> 82.5 us
  starting transfers between devices: 248 us -> 299 us
    all_gather x1 -> x0, waiting for transfers between devices: 188 us -> none  [ice_work(): lax.all_gather(adj_z, 'ice', axis=1, tiled=True)]
    all_to_all x1, blocking collectives: 5.32 us -> 79.6 us  [shards(): lax.all_to_all(outgoing, 'ocean', split_axis=0, concat_axis=0, tiled=True)]
    all_to_all x0 -> x1, starting transfers between devices: none -> 50.5 us  [switch_views(): all_to_all(jnp.tile(here_x, vals), chip_axis, split_axis=1, concat_axis=1...]
    all_to_all x0 -> x1, waiting for transfers between devices: none -> 30.4 us  [switch_views(): all_to_all(jnp.tile(here_x, vals), chip_axis, split_axis=1, concat_axis=1...]
where the time goes in v1:
time: 694 us; the launch traced here: 691 us
  starting transfers between devices  299 us (43%)
  waiting for transfers between devices  246 us (35%)
  blocking collectives  82.5 us (12%)
  local copies, waits for them, and re-layouts  19.7 us (3%)
  other arithmetic  17.5 us (3%)
  between operations  14.4 us (2%)
  matrix products  9.91 us (1%)
    ppermute x64, starting transfers between devices, passed_along(): return lax.ppermute(block, axis, route)  238 us
    ppermute x64, waiting for transfers between devices, passed_along(): return lax.ppermute(block, axis, route)  138 us
    all_to_all x1, blocking collectives, shards(): lax.all_to_all(outgoing, 'ocean', split_axis=0, concat_axis=0, tiled=True)  79.6 us
    all_gather x1, waiting for transfers between devices, ice_work(): lax.all_gather(source, 'ice', axis=1, tiled=True)  77.3 us
    all_to_all x1, starting transfers between devices, switch_views(): all_to_all(jnp.tile(here_x, vals), chip_axis, split_axis=1, concat_axis=1...  50.5 us
    all_to_all x1, waiting for transfers between devices, switch_views(): all_to_all(jnp.tile(here_x, vals), chip_axis, split_axis=1, concat_axis=1...  30.4 us
  transfers between devices with their start and end apart: 69, of which 66 were waited for; matrix products, arithmetic and copies ran while one was open for 2% of the time, Pallas kernels for 0%

profile of v1, /device:TPU:1, one launch (start us, length us, event | category | flops | bytes accessed | tf_op | source)
XLA Modules:
  0.0 691.2 jit_solution(13407873215545136583)
XLA Ops:
  45.0 77.3 %all-gather.3.cloned.1.call-done = f32[16,1,512,128]{3,2,0,1:T(8,128)} async-done(((f32[16,1,8,128]{3,2,0,1:T(8,128)}), f32[16,1,512,128]{3,2,0,1:T(8,128)}) %all-gather.3.cloned.1.call-update) | async-done | bytes 4194320 | tf_op jit(solution)/shard_map/all_gather | solution.py:55
  126.8 84.1 %while.84 = (s32[]{:T(128)}, f32[16,8,128]{2,1,0:T(8,128)S(1)}, f32[16,8,128]{2,1,0:T(8,128)S(1)}, f32[8,16,8,128]{3,2,1,0:T(8,128)S(1)}, f32[16,8,128]{2,1,0:T(...) while((s32[]{:T(128)}, f32[16,8,128]{2,1,0:T(8,128)S(1)}, f32[16,8,128]{2,1,0:T(8,128)S(1)}, ...), condition=%wide.region_7.8_spmd, body=%wide.region_6.7_spmd.sunk | while | flops 262146 | bytes 1073313 | solution.py:72
  211.1 90.0 %while.85 = (s32[]{:T(128)}, f32[16,8,128]{2,1,0:T(8,128)S(1)}, f32[16,8,128]{2,1,0:T(8,128)S(1)}, f32[8,16,8,128]{3,2,1,0:T(8,128)S(1)}, f32[16,8,128]{2,1,0:T(...) while((s32[]{:T(128)}, f32[16,8,128]{2,1,0:T(8,128)S(1)}, f32[16,8,128]{2,1,0:T(8,128)S(1)}, ...), condition=%wide.region_9.10_spmd, body=%wide.region_8.9_spmd.sunk | while | flops 262146 | bytes 1073313 | solution.py:72
  301.0 104.9 %while.87 = (s32[]{:T(128)}, f32[16,8,128]{2,1,0:T(8,128)S(1)}, f32[16,8,128]{2,1,0:T(8,128)S(1)}, f32[16,8,128]{2,1,0:T(8,128)S(1)}, f32[16,8,128]{2,1,0:T(8,12...) while((s32[]{:T(128)}, f32[16,8,128]{2,1,0:T(8,128)S(1)}, ...), condition=%wide.region_11.12_spmd.clone, body=%wide.region_10.11_spmd.clone.sunk | while | flops 327684 | bytes 1327311 | solution.py:87
  312.8 7.3 %collective-permute-start.6 = (f32[16,1,128]{2,1,0:T(1,128)S(1)}, f32[16,1,128]{2,1,0:T(1,128)S(1)}, u32[]{:S(2)}, u32[]{:S(2)}) collective-permute-start(f32[16,1,128]{2,1,0:T(1,128)S(1)} %slice.355), channel_id=1, source_target_pairs={{0,1},{1,2},{2,3},{3,4},{4,5},{5,6},{6,7},{7,8},{8,9},{9,10},{10,1... | collective-permute-start | bytes 24584 | tf_op jit(solution)/shard_map/while/body/eval_jaxpr/ppermute | solution.py:19
  326.3 7.1 %collective-permute-start.6 = (f32[16,1,128]{2,1,0:T(1,128)S(1)}, f32[16,1,128]{2,1,0:T(1,128)S(1)}, u32[]{:S(2)}, u32[]{:S(2)}) collective-permute-start(f32[16,1,128]{2,1,0:T(1,128)S(1)} %slice.355), channel_id=1, source_target_pairs={{0,1},{1,2},{2,3},{3,4},{4,5},{5,6},{6,7},{7,8},{8,9},{9,10},{10,1... | collective-permute-start | bytes 24584 | tf_op jit(solution)/shard_map/while/body/eval_jaxpr/ppermute | solution.py:19
  339.1 7.8 %collective-permute-start.6 = (f32[16,1,128]{2,1,0:T(1,128)S(1)}, f32[16,1,128]{2,1,0:T(1,128)S(1)}, u32[]{:S(2)}, u32[]{:S(2)}) collective-permute-start(f32[16,1,128]{2,1,0:T(1,128)S(1)} %slice.355), channel_id=1, source_target_pairs={{0,1},{1,2},{2,3},{3,4},{4,5},{5,6},{6,7},{7,8},{8,9},{9,10},{10,1... | collective-permute-start | bytes 24584 | tf_op jit(solution)/shard_map/while/body/eval_jaxpr/ppermute | solution.py:19
  352.6 7.4 %collective-permute-start.6 = (f32[16,1,128]{2,1,0:T(1,128)S(1)}, f32[16,1,128]{2,1,0:T(1,128)S(1)}, u32[]{:S(2)}, u32[]{:S(2)}) collective-permute-start(f32[16,1,128]{2,1,0:T(1,128)S(1)} %slice.355), channel_id=1, source_target_pairs={{0,1},{1,2},{2,3},{3,4},{4,5},{5,6},{6,7},{7,8},{8,9},{9,10},{10,1... | collective-permute-start | bytes 24584 | tf_op jit(solution)/shard_map/while/body/eval_jaxpr/ppermute | solution.py:19
  365.9 7.6 %collective-permute-start.6 = (f32[16,1,128]{2,1,0:T(1,128)S(1)}, f32[16,1,128]{2,1,0:T(1,128)S(1)}, u32[]{:S(2)}, u32[]{:S(2)}) collective-permute-start(f32[16,1,128]{2,1,0:T(1,128)S(1)} %slice.355), channel_id=1, source_target_pairs={{0,1},{1,2},{2,3},{3,4},{4,5},{5,6},{6,7},{7,8},{8,9},{9,10},{10,1... | collective-permute-start | bytes 24584 | tf_op jit(solution)/shard_map/while/body/eval_jaxpr/ppermute | solution.py:19
  379.5 7.2 %collective-permute-start.6 = (f32[16,1,128]{2,1,0:T(1,128)S(1)}, f32[16,1,128]{2,1,0:T(1,128)S(1)}, u32[]{:S(2)}, u32[]{:S(2)}) collective-permute-start(f32[16,1,128]{2,1,0:T(1,128)S(1)} %slice.355), channel_id=1, source_target_pairs={{0,1},{1,2},{2,3},{3,4},{4,5},{5,6},{6,7},{7,8},{8,9},{9,10},{10,1... | collective-permute-start | bytes 24584 | tf_op jit(solution)/shard_map/while/body/eval_jaxpr/ppermute | solution.py:19
  392.7 7.3 %collective-permute-start.6 = (f32[16,1,128]{2,1,0:T(1,128)S(1)}, f32[16,1,128]{2,1,0:T(1,128)S(1)}, u32[]{:S(2)}, u32[]{:S(2)}) collective-permute-start(f32[16,1,128]{2,1,0:T(1,128)S(1)} %slice.355), channel_id=1, source_target_pairs={{0,1},{1,2},{2,3},{3,4},{4,5},{5,6},{6,7},{7,8},{8,9},{9,10},{10,1... | collective-permute-start | bytes 24584 | tf_op jit(solution)/shard_map/while/body/eval_jaxpr/ppermute | solution.py:19
  406.0 107.0 %while.86 = (s32[]{:T(128)}, f32[16,8,128]{2,1,0:T(8,128)S(1)}, f32[16,8,128]{2,1,0:T(8,128)S(1)}, f32[16,8,128]{2,1,0:T(8,128)S(1)}, f32[16,8,128]{2,1,0:T(8,12...) while((s32[]{:T(128)}, f32[16,8,128]{2,1,0:T(8,128)S(1)}, ...), condition=%wide.region_13.14_spmd, body=%wide.region_12.13_spmd.sunk | while | flops 294915 | bytes 1327293 | solution.py:87
  406.0 7.6 %collective-permute-start.4 = (f32[16,1,128]{2,1,0:T(1,128)S(1)}, f32[16,1,128]{2,1,0:T(1,128)S(1)}, u32[]{:S(2)}, u32[]{:S(2)}) collective-permute-start(f32[16,1,128]{2,1,0:T(1,128)S(1)} %slice.351), channel_id=1, source_target_pairs={{0,1},{1,2},{2,3},{3,4},{4,5},{5,6},{6,7},{7,8},{8,9},{9,10},{10,1... | collective-permute-start | bytes 24584 | tf_op jit(solution)/shard_map/while/body/eval_jaxpr/ppermute | solution.py:19
  419.6 7.3 %collective-permute-start.4 = (f32[16,1,128]{2,1,0:T(1,128)S(1)}, f32[16,1,128]{2,1,0:T(1,128)S(1)}, u32[]{:S(2)}, u32[]{:S(2)}) collective-permute-start(f32[16,1,128]{2,1,0:T(1,128)S(1)} %slice.351), channel_id=1, source_target_pairs={{0,1},{1,2},{2,3},{3,4},{4,5},{5,6},{6,7},{7,8},{8,9},{9,10},{10,1... | collective-permute-start | bytes 24584 | tf_op jit(solution)/shard_map/while/body/eval_jaxpr/ppermute | solution.py:19
  432.8 7.6 %collective-permute-start.4 = (f32[16,1,128]{2,1,0:T(1,128)S(1)}, f32[16,1,128]{2,1,0:T(1,128)S(1)}, u32[]{:S(2)}, u32[]{:S(2)}) collective-permute-start(f32[16,1,128]{2,1,0:T(1,128)S(1)} %slice.351), channel_id=1, source_target_pairs={{0,1},{1,2},{2,3},{3,4},{4,5},{5,6},{6,7},{7,8},{8,9},{9,10},{10,1... | collective-permute-start | bytes 24584 | tf_op jit(solution)/shard_map/while/body/eval_jaxpr/ppermute | solution.py:19
  446.1 7.3 %collective-permute-start.4 = (f32[16,1,128]{2,1,0:T(1,128)S(1)}, f32[16,1,128]{2,1,0:T(1,128)S(1)}, u32[]{:S(2)}, u32[]{:S(2)}) collective-permute-start(f32[16,1,128]{2,1,0:T(1,128)S(1)} %slice.351), channel_id=1, source_target_pairs={{0,1},{1,2},{2,3},{3,4},{4,5},{5,6},{6,7},{7,8},{8,9},{9,10},{10,1... | collective-permute-start | bytes 24584 | tf_op jit(solution)/shard_map/while/body/eval_jaxpr/ppermute | solution.py:19
  459.4 7.6 %collective-permute-start.4 = (f32[16,1,128]{2,1,0:T(1,128)S(1)}, f32[16,1,128]{2,1,0:T(1,128)S(1)}, u32[]{:S(2)}, u32[]{:S(2)}) collective-permute-start(f32[16,1,128]{2,1,0:T(1,128)S(1)} %slice.351), channel_id=1, source_target_pairs={{0,1},{1,2},{2,3},{3,4},{4,5},{5,6},{6,7},{7,8},{8,9},{9,10},{10,1... | collective-permute-start | bytes 24584 | tf_op jit(solution)/shard_map/while/body/eval_jaxpr/ppermute | solution.py:19
  473.0 7.2 %collective-permute-start.4 = (f32[16,1,128]{2,1,0:T(1,128)S(1)}, f32[16,1,128]{2,1,0:T(1,128)S(1)}, u32[]{:S(2)}, u32[]{:S(2)}) collective-permute-start(f32[16,1,128]{2,1,0:T(1,128)S(1)} %slice.351), channel_id=1, source_target_pairs={{0,1},{1,2},{2,3},{3,4},{4,5},{5,6},{6,7},{7,8},{8,9},{9,10},{10,1... | collective-permute-start | bytes 24584 | tf_op jit(solution)/shard_map/while/body/eval_jaxpr/ppermute | solution.py:19
  486.2 7.3 %collective-permute-start.4 = (f32[16,1,128]{2,1,0:T(1,128)S(1)}, f32[16,1,128]{2,1,0:T(1,128)S(1)}, u32[]{:S(2)}, u32[]{:S(2)}) collective-permute-start(f32[16,1,128]{2,1,0:T(1,128)S(1)} %slice.351), channel_id=1, source_target_pairs={{0,1},{1,2},{2,3},{3,4},{4,5},{5,6},{6,7},{7,8},{8,9},{9,10},{10,1... | collective-permute-start | bytes 24584 | tf_op jit(solution)/shard_map/while/body/eval_jaxpr/ppermute | solution.py:19
  500.1 7.0 %collective-permute-start.4 = (f32[16,1,128]{2,1,0:T(1,128)S(1)}, f32[16,1,128]{2,1,0:T(1,128)S(1)}, u32[]{:S(2)}, u32[]{:S(2)}) collective-permute-start(f32[16,1,128]{2,1,0:T(1,128)S(1)} %slice.351), channel_id=1, source_target_pairs={{0,1},{1,2},{2,3},{3,4},{4,5},{5,6},{6,7},{7,8},{8,9},{9,10},{10,1... | collective-permute-start | bytes 24584 | tf_op jit(solution)/shard_map/while/body/eval_jaxpr/ppermute | solution.py:19
  515.5 50.5 %all-to-all-start.3 = ((f32[16,512,128]{2,0,1:T(8,128)}), f32[16,512,128]{2,0,1:T(8,128)}, u32[]{:S(2)}, u32[]{:S(2)}) async-start(f32[16,512,128]{2,0,1:T(8,128)} %bitcast.129), calls=%async_computation.3 | async-start | bytes 8388608 | tf_op jit(solution)/shard_map/all_to_all | solution.py:96
  566.1 30.4 %all-to-all-done.3 = f32[16,512,128]{2,0,1:T(8,128)} async-done(((f32[16,512,128]{2,0,1:T(8,128)}), f32[16,512,128]{2,0,1:T(8,128)}, u32[]{:S(2)}, u32[]{:S(2)}) %all-to-all-start.3) | async-done | bytes 4194336 | tf_op jit(solution)/shard_map/all_to_all | solution.py:96
  596.5 5.5 fusion.29
  602.8 79.6 %all_to_all.30 = f32[32,4,8,128]{3,2,1,0:T(8,128)S(1)} all-to-all(f32[32,4,8,128]{3,2,1,0:T(8,128)S(1)} %select_multiply_fusion.1), channel_id=1, replica_groups=mesh['ocean'=2,'ice'=64] {'ocean'}, dimensions={0} | all-to-all | bytes 1048576 | tf_op jit(solution)/shard_map/all_to_all | solution.py:162
  (390 shorter events, 321.7 us)
Async XLA Ops:
  16.8 16.8 %all-to-all-start = ((f32[2,16,1]{1,2,0:T(1,128)}), f32[2,16,1]{1,2,0:T(1,128)S(1)}, u32[]{:S(2)}, u32[]{:S(2)}) async-start(f32[2,16,1]{1,2,0:T(1,128)} %bitcast.7), calls=%async_computation | async-start | bytes 2048 | tf_op jit(solution)/shard_map/all_to_all | solution.py:138
  41.6 80.7 %all-gather.3.cloned.1.call-start = ((), (), s32[]{:S(2)}) async-start(), calls=%async_computation.5 | async-start | bytes 4259840 | tf_op jit(solution)/shard_map/all_gather | solution.py:55
  154.8 6.3 collective-permute-start
  166.2 6.3 collective-permute-start
  222.3 6.3 collective-permute-start.2
  244.9 6.3 collective-permute-start.2
  267.3 6.3 collective-permute-start.2
  301.1 6.3 collective-permute-start.6
  312.8 8.1 %collective-permute-start.6 = (f32[16,1,128]{2,1,0:T(1,128)S(1)}, f32[16,1,128]{2,1,0:T(1,128)S(1)}, u32[]{:S(2)}, u32[]{:S(2)}) collective-permute-start(f32[16,1,128]{2,1,0:T(1,128)S(1)} %slice.355), channel_id=1, source_target_pairs={{0,1},{1,2},{2,3},{3,4},{4,5},{5,6},{6,7},{7,8},{8,9},{9,10},{10,1... | collective-permute-start | bytes 24584 | tf_op jit(solution)/shard_map/while/body/eval_jaxpr/ppermute | solution.py:19
  326.3 7.8 %collective-permute-start.6 = (f32[16,1,128]{2,1,0:T(1,128)S(1)}, f32[16,1,128]{2,1,0:T(1,128)S(1)}, u32[]{:S(2)}, u32[]{:S(2)}) collective-permute-start(f32[16,1,128]{2,1,0:T(1,128)S(1)} %slice.355), channel_id=1, source_target_pairs={{0,1},{1,2},{2,3},{3,4},{4,5},{5,6},{6,7},{7,8},{8,9},{9,10},{10,1... | collective-permute-start | bytes 24584 | tf_op jit(solution)/shard_map/while/body/eval_jaxpr/ppermute | solution.py:19
  339.1 8.6 %collective-permute-start.6 = (f32[16,1,128]{2,1,0:T(1,128)S(1)}, f32[16,1,128]{2,1,0:T(1,128)S(1)}, u32[]{:S(2)}, u32[]{:S(2)}) collective-permute-start(f32[16,1,128]{2,1,0:T(1,128)S(1)} %slice.355), channel_id=1, source_target_pairs={{0,1},{1,2},{2,3},{3,4},{4,5},{5,6},{6,7},{7,8},{8,9},{9,10},{10,1... | collective-permute-start | bytes 24584 | tf_op jit(solution)/shard_map/while/body/eval_jaxpr/ppermute | solution.py:19
  352.6 8.1 %collective-permute-start.6 = (f32[16,1,128]{2,1,0:T(1,128)S(1)}, f32[16,1,128]{2,1,0:T(1,128)S(1)}, u32[]{:S(2)}, u32[]{:S(2)}) collective-permute-start(f32[16,1,128]{2,1,0:T(1,128)S(1)} %slice.355), channel_id=1, source_target_pairs={{0,1},{1,2},{2,3},{3,4},{4,5},{5,6},{6,7},{7,8},{8,9},{9,10},{10,1... | collective-permute-start | bytes 24584 | tf_op jit(solution)/shard_map/while/body/eval_jaxpr/ppermute | solution.py:19
  365.9 8.4 %collective-permute-start.6 = (f32[16,1,128]{2,1,0:T(1,128)S(1)}, f32[16,1,128]{2,1,0:T(1,128)S(1)}, u32[]{:S(2)}, u32[]{:S(2)}) collective-permute-start(f32[16,1,128]{2,1,0:T(1,128)S(1)} %slice.355), channel_id=1, source_target_pairs={{0,1},{1,2},{2,3},{3,4},{4,5},{5,6},{6,7},{7,8},{8,9},{9,10},{10,1... | collective-permute-start | bytes 24584 | tf_op jit(solution)/shard_map/while/body/eval_jaxpr/ppermute | solution.py:19
  379.5 8.0 %collective-permute-start.6 = (f32[16,1,128]{2,1,0:T(1,128)S(1)}, f32[16,1,128]{2,1,0:T(1,128)S(1)}, u32[]{:S(2)}, u32[]{:S(2)}) collective-permute-start(f32[16,1,128]{2,1,0:T(1,128)S(1)} %slice.355), channel_id=1, source_target_pairs={{0,1},{1,2},{2,3},{3,4},{4,5},{5,6},{6,7},{7,8},{8,9},{9,10},{10,1... | collective-permute-start | bytes 24584 | tf_op jit(solution)/shard_map/while/body/eval_jaxpr/ppermute | solution.py:19
  392.7 8.0 %collective-permute-start.6 = (f32[16,1,128]{2,1,0:T(1,128)S(1)}, f32[16,1,128]{2,1,0:T(1,128)S(1)}, u32[]{:S(2)}, u32[]{:S(2)}) collective-permute-start(f32[16,1,128]{2,1,0:T(1,128)S(1)} %slice.355), channel_id=1, source_target_pairs={{0,1},{1,2},{2,3},{3,4},{4,5},{5,6},{6,7},{7,8},{8,9},{9,10},{10,1... | collective-permute-start | bytes 24584 | tf_op jit(solution)/shard_map/while/body/eval_jaxpr/ppermute | solution.py:19
  406.0 8.4 %collective-permute-start.4 = (f32[16,1,128]{2,1,0:T(1,128)S(1)}, f32[16,1,128]{2,1,0:T(1,128)S(1)}, u32[]{:S(2)}, u32[]{:S(2)}) collective-permute-start(f32[16,1,128]{2,1,0:T(1,128)S(1)} %slice.351), channel_id=1, source_target_pairs={{0,1},{1,2},{2,3},{3,4},{4,5},{5,6},{6,7},{7,8},{8,9},{9,10},{10,1... | collective-permute-start | bytes 24584 | tf_op jit(solution)/shard_map/while/body/eval_jaxpr/ppermute | solution.py:19
  419.6 8.1 %collective-permute-start.4 = (f32[16,1,128]{2,1,0:T(1,128)S(1)}, f32[16,1,128]{2,1,0:T(1,128)S(1)}, u32[]{:S(2)}, u32[]{:S(2)}) collective-permute-start(f32[16,1,128]{2,1,0:T(1,128)S(1)} %slice.351), channel_id=1, source_target_pairs={{0,1},{1,2},{2,3},{3,4},{4,5},{5,6},{6,7},{7,8},{8,9},{9,10},{10,1... | collective-permute-start | bytes 24584 | tf_op jit(solution)/shard_map/while/body/eval_jaxpr/ppermute | solution.py:19
  432.8 8.4 %collective-permute-start.4 = (f32[16,1,128]{2,1,0:T(1,128)S(1)}, f32[16,1,128]{2,1,0:T(1,128)S(1)}, u32[]{:S(2)}, u32[]{:S(2)}) collective-permute-start(f32[16,1,128]{2,1,0:T(1,128)S(1)} %slice.351), channel_id=1, source_target_pairs={{0,1},{1,2},{2,3},{3,4},{4,5},{5,6},{6,7},{7,8},{8,9},{9,10},{10,1... | collective-permute-start | bytes 24584 | tf_op jit(solution)/shard_map/while/body/eval_jaxpr/ppermute | solution.py:19
  446.1 8.1 %collective-permute-start.4 = (f32[16,1,128]{2,1,0:T(1,128)S(1)}, f32[16,1,128]{2,1,0:T(1,128)S(1)}, u32[]{:S(2)}, u32[]{:S(2)}) collective-permute-start(f32[16,1,128]{2,1,0:T(1,128)S(1)} %slice.351), channel_id=1, source_target_pairs={{0,1},{1,2},{2,3},{3,4},{4,5},{5,6},{6,7},{7,8},{8,9},{9,10},{10,1... | collective-permute-start | bytes 24584 | tf_op jit(solution)/shard_map/while/body/eval_jaxpr/ppermute | solution.py:19
  459.4 8.4 %collective-permute-start.4 = (f32[16,1,128]{2,1,0:T(1,128)S(1)}, f32[16,1,128]{2,1,0:T(1,128)S(1)}, u32[]{:S(2)}, u32[]{:S(2)}) collective-permute-start(f32[16,1,128]{2,1,0:T(1,128)S(1)} %slice.351), channel_id=1, source_target_pairs={{0,1},{1,2},{2,3},{3,4},{4,5},{5,6},{6,7},{7,8},{8,9},{9,10},{10,1... | collective-permute-start | bytes 24584 | tf_op jit(solution)/shard_map/while/body/eval_jaxpr/ppermute | solution.py:19
  473.0 8.0 %collective-permute-start.4 = (f32[16,1,128]{2,1,0:T(1,128)S(1)}, f32[16,1,128]{2,1,0:T(1,128)S(1)}, u32[]{:S(2)}, u32[]{:S(2)}) collective-permute-start(f32[16,1,128]{2,1,0:T(1,128)S(1)} %slice.351), channel_id=1, source_target_pairs={{0,1},{1,2},{2,3},{3,4},{4,5},{5,6},{6,7},{7,8},{8,9},{9,10},{10,1... | collective-permute-start | bytes 24584 | tf_op jit(solution)/shard_map/while/body/eval_jaxpr/ppermute | solution.py:19
  486.2 8.1 %collective-permute-start.4 = (f32[16,1,128]{2,1,0:T(1,128)S(1)}, f32[16,1,128]{2,1,0:T(1,128)S(1)}, u32[]{:S(2)}, u32[]{:S(2)}) collective-permute-start(f32[16,1,128]{2,1,0:T(1,128)S(1)} %slice.351), channel_id=1, source_target_pairs={{0,1},{1,2},{2,3},{3,4},{4,5},{5,6},{6,7},{7,8},{8,9},{9,10},{10,1... | collective-permute-start | bytes 24584 | tf_op jit(solution)/shard_map/while/body/eval_jaxpr/ppermute | solution.py:19
  500.1 7.8 %collective-permute-start.4 = (f32[16,1,128]{2,1,0:T(1,128)S(1)}, f32[16,1,128]{2,1,0:T(1,128)S(1)}, u32[]{:S(2)}, u32[]{:S(2)}) collective-permute-start(f32[16,1,128]{2,1,0:T(1,128)S(1)} %slice.351), channel_id=1, source_target_pairs={{0,1},{1,2},{2,3},{3,4},{4,5},{5,6},{6,7},{7,8},{8,9},{9,10},{10,1... | collective-permute-start | bytes 24584 | tf_op jit(solution)/shard_map/while/body/eval_jaxpr/ppermute | solution.py:19
  515.5 81.0 %all-to-all-start.3 = ((f32[16,512,128]{2,0,1:T(8,128)}), f32[16,512,128]{2,0,1:T(8,128)}, u32[]{:S(2)}, u32[]{:S(2)}) async-start(f32[16,512,128]{2,0,1:T(8,128)} %bitcast.129), calls=%async_computation.3 | async-start | bytes 8388608 | tf_op jit(solution)/shard_map/all_to_all | solution.py:96
  (51 other events, 436.1 us)
Sparse Core Ops, SparseCore 0:
  45.7 76.5 all-gather.2
